TPU v7x, 512 devices: a whole 4x8x8 slice. The times are simulated.
512 devices in a mesh: dp: 16 (over z, x_lo), space: 32 (over y, x_hi, core).
Axes of the slice: x: 4 (x_hi: 2, x_lo: 2; x = x_hi * 2 + x_lo), y: 8, z: 8, core: 2. Of those that a mesh axis runs over, the one named last changes fastest.
Arguments:
- features: bfloat16 [16, 64, 72, 2048], P('dp', 'space'), may hold values from -150 to 150
- depthwise: bfloat16 [2, 9, 2048], replicated, may hold values from -2 to 2
- pointwise: bfloat16 [2048, 512], replicated, may hold values from -0.125 to 0.125
- bn_gain: float32 [2, 2048], replicated, may hold values from 0.1 to 1.9
- cotangent: bfloat16 [16, 64, 72, 256], P('dp', 'space'), may hold values from -6 to 6
Outputs:
- block_out: bfloat16 [16, 64, 72, 256], P('dp', 'space')
- grad_pointwise: float32 [2048, 512], P('space')
- grad_depthwise: float32 [2, 9, 2048], P(None, None, 'space')
All inputs are finite; a program needn't handle non-finite values.
Results may differ from a plain program's by a relative error of at most 0.001.
The roundings to bfloat16 on the way count: a program that leaves them out, or rounds other values in their place, can miss the bound.
Values may be sent and summed in bfloat16 or wider, within the bound.
No kernel may reach another device: no remote copies, remote signals or barrier semaphores. Data moves between devices by JAX's collectives and lax.ppermute only.
A program may use at most 64 MiB of HBM per device.

v0:
```python
import jax
import jax.numpy as jnp
from jax import lax
from jax.sharding import PartitionSpec as P

NEAR_DILATION = 12
FAR_DILATION = 24
eps_norm = 1e-05


def shifted(value, axis, steps):
    count = lax.axis_size(axis)
    leading, last = (max(0, -steps), min(count, count - steps))
    return lax.ppermute(value, axis, [(source, source + steps) for source in range(leading, last)])


def shift_dim(input_values, offset, reduce_axis):
    if offset == 0:
        return input_values
    extent = abs(offset)
    length_here = input_values.shape[reduce_axis]
    padding = [(0, 0)] * input_values.ndim
    padding[reduce_axis] = (extent, extent)
    padded = jnp.pad(input_values, padding)
    return lax.slice_in_dim(
        padded, extent + offset, extent + offset + length_here, axis=reduce_axis
    )


def depthwise_out(sources, weights, dilation, col_axis):
    running_total = jnp.zeros(sources[1].shape, jnp.float32)
    for row_tap in range(3):
        for col_tap in range(3):
            moved = shift_dim(sources[row_tap], (col_tap - 1) * dilation, col_axis)
            running_total = running_total + weights[3 * row_tap + col_tap].astype(
                jnp.float32
            ) * moved.astype(jnp.float32)
    return running_total


def depthwise_grad(sources, gradient_map, dilation, col_axis, sum_axes):
    results = []
    for row_tap in range(3):
        for col_tap in range(3):
            moved = shift_dim(sources[row_tap], (col_tap - 1) * dilation, col_axis)
            results.append(
                jnp.sum(gradient_map.astype(jnp.float32) * moved.astype(jnp.float32), axis=sum_axes)
            )
    return jnp.stack(results)


def remote_sources(features, dilation):
    row_count = features.shape[1]
    steps_away = dilation // row_count
    above = shifted(features, "space", steps_away)
    below = shifted(features, "space", -steps_away)
    return (above, features, below)


def body(features, depthwise, pointwise, bn_gain, cotangent):
    dilation_rates = (NEAR_DILATION, FAR_DILATION)
    row_count = features.shape[1]
    map_width = features.shape[2]
    channels = features.shape[3]
    out_width = pointwise.shape[1] // 2
    space_count = lax.axis_size("space")
    sample_count = lax.axis_size("dp")
    chan_share = channels // space_count
    position = lax.axis_index("space")
    pixels = row_count * map_width
    count = float(sample_count * space_count * row_count * map_width)
    sources = [remote_sources(features, dilation_rates[k]) for k in range(2)]
    branch_vals = jnp.stack(
        [depthwise_out(sources[k], depthwise[k], dilation_rates[k], 2) for k in range(2)]
    ).astype(jnp.bfloat16)
    input_values = branch_vals.astype(jnp.float32)
    sum_vals, sum_squares = lax.psum(
        (
            jnp.sum(input_values, axis=(1, 2, 3)),
            jnp.sum(input_values * input_values, axis=(1, 2, 3)),
        ),
        ("dp", "space"),
    )
    batch_average = sum_vals / count
    variance = sum_squares / count - batch_average * batch_average
    inverse_deviation = lax.rsqrt(variance + eps_norm)[:, None, None, None, :]
    norm_gains = bn_gain[:, None, None, None, :]
    normalized_input = (input_values - batch_average[:, None, None, None, :]) * inverse_deviation
    scaled_values = norm_gains * normalized_input
    used = jnp.maximum(scaled_values, 0.0).astype(jnp.bfloat16)
    flattened_used = used.reshape(2, pixels, channels)
    gradient_rows = cotangent.reshape(pixels, out_width)
    branch_output = jnp.dot(
        flattened_used[0], pointwise[:, :out_width], preferred_element_type=jnp.float32
    ) + jnp.dot(flattened_used[1], pointwise[:, out_width:], preferred_element_type=jnp.float32)
    block_out = branch_output.astype(jnp.bfloat16).reshape(1, row_count, map_width, out_width)
    pieces = []
    for branch_no in range(2):
        columns = flattened_used[branch_no]
        pieces.append(
            lax.dot_general(
                columns, gradient_rows, (((0,), (0,)), ((), ())), preferred_element_type=jnp.float32
            )
        )
    snapshot_grad = lax.psum_scatter(
        jnp.concatenate(pieces, axis=1), "space", scatter_dimension=0, tiled=True
    )
    grad_pw = lax.psum(snapshot_grad, "dp")
    grad_used = jnp.stack(
        [
            lax.dot_general(
                gradient_rows,
                pointwise[:, k * out_width : (k + 1) * out_width],
                (((1,), (1,)), ((), ())),
                preferred_element_type=jnp.float32,
            )
            for k in range(2)
        ]
    )
    grad_used = grad_used.reshape(2, 1, row_count, map_width, channels)
    normalized_gradient = jnp.where(scaled_values > 0, grad_used, 0.0) * norm_gains
    first_sums, second_sums = lax.psum(
        (
            jnp.sum(normalized_gradient, axis=(1, 2, 3)),
            jnp.sum(normalized_gradient * normalized_input, axis=(1, 2, 3)),
        ),
        ("dp", "space"),
    )
    mean_first_moment = (first_sums / count)[:, None, None, None, :]
    mean_second_moment = (second_sums / count)[:, None, None, None, :]
    gradient_values = (
        inverse_deviation
        * (normalized_gradient - mean_first_moment - normalized_input * mean_second_moment)
    ).astype(jnp.bfloat16)
    local_grads = jnp.stack(
        [
            depthwise_grad(sources[k], gradient_values[k], dilation_rates[k], 2, (0, 1, 2))
            for k in range(2)
        ]
    )
    summed = lax.psum(local_grads, ("dp", "space"))
    grad_dw = lax.dynamic_slice_in_dim(summed, position * chan_share, chan_share, 2)
    return (block_out, grad_pw, grad_dw)


def solution(mesh):
    in_specs = (P("dp", "space", None, None), P(), P(), P(), P("dp", "space", None, None))
    out_specs = (P("dp", "space", None, None), P("space", None), P(None, None, "space"))
    return jax.shard_map(body, mesh=mesh, in_specs=in_specs, out_specs=out_specs, check_vma=False)
```

profile of v0, /device:TPU:2, one launch (start us, length us, event | category | flops | bytes accessed | tf_op | source)
XLA Modules:
  0.0 725.3 jit_solution(8803910029780150236)
XLA Ops:
  8.0 0.0 copy-start
  8.0 0.0 reduce-scatter.4.cloned.1.call-start
  8.1 5.7 collective-permute-start.2
  13.8 1.3 collective-permute-start.1
  15.1 7.0 collective-permute-start
  22.1 1.3 collective-permute-start.3
  23.4 1.7 convolution_bitcast_fusion
  25.1 0.1 slice_convert_fusion.17
  25.2 0.5 convolution_bitcast_fusion.1
  25.7 7.6 %collective-permute-done.1 = bf16[1,2,72,2048]{3,2,1,0:T(8,128)(2,1)S(1)} collective-permute-done((bf16[1,2,72,2048]{3,2,1,0:T(8,128)(2,1)}, bf16[1,2,72,2048]{3,2,1,0:T(8,128)(2,1)S(1)}, u32[]{:S(2)}, u32[]{:S(2)}) %collective-permute-start.1) | collective-permute-done | bytes 589856 | tf_op jit(solution)/shard_map/ppermute | solution.py:14
  33.3 11.6 %collective-permute-done = bf16[1,2,72,2048]{3,2,1,0:T(8,128)(2,1)S(1)} collective-permute-done((bf16[1,2,72,2048]{3,2,1,0:T(8,128)(2,1)}, bf16[1,2,72,2048]{3,2,1,0:T(8,128)(2,1)S(1)}, u32[]{:S(2)}, u32[]{:S(2)}) %collective-permute-start) | collective-permute-done | bytes 589856 | tf_op jit(solution)/shard_map/ppermute | solution.py:14
  44.9 1.1 fusion.58
  46.1 25.9 %collective-permute-done.3 = bf16[1,2,72,2048]{3,2,1,0:T(8,128)(2,1)S(1)} collective-permute-done((bf16[1,2,72,2048]{3,2,1,0:T(8,128)(2,1)}, bf16[1,2,72,2048]{3,2,1,0:T(8,128)(2,1)S(1)}, u32[]{:S(2)}, u32[]{:S(2)}) %collective-permute-start.3) | collective-permute-done | bytes 589856 | tf_op jit(solution)/shard_map/ppermute | solution.py:14
  72.0 0.8 fusion.57
  72.9 0.8 copy-done.2
  73.7 0.4 convert_reduce_fusion
  74.1 121.6 %all-reduce.7 = (f32[2,2048]{1,0:T(2,128)S(1)}, f32[2,2048]{1,0:T(2,128)S(1)}) all-reduce(f32[2,2048]{1,0:T(2,128)S(1)} %get-tuple-element.42, f32[2,2048]{1,0:T(2,128)S(1)} %get-tuple-element.41), channel_id=1, replica_groups=mesh['dp'=16,'space'=32] {'dp','space'}, use_global_device_ids=true, to_apply=%region_3.4 | all-reduce | flops 8192 | bytes 65536 | tf_op jit(solution)/shard_map/psum | solution.py:77
  195.7 2.0 fusion.61
  197.7 93.1 %all-reduce.6 = (f32[2,2048]{1,0:T(2,128)S(1)}, f32[2,2048]{1,0:T(2,128)S(1)}) all-reduce(f32[2,2048]{1,0:T(2,128)S(1)} %get-tuple-element.13, f32[2,2048]{1,0:T(2,128)S(1)} %get-tuple-element.12), channel_id=1, replica_groups=mesh['dp'=16,'space'=32] {'dp','space'}, use_global_device_ids=true, to_apply=%region_9.10 | all-reduce | flops 8192 | bytes 65536 | tf_op jit(solution)/shard_map/psum | solution.py:122
  290.8 3.2 fusion.10
  294.0 0.1 fusion.62
  294.1 0.5 fusion.64
  294.6 0.3 copy-done.13
  294.9 0.5 fusion.63
  295.4 2.5 pad_maximum_fusion
  297.9 5.3 copy.13
  303.2 0.0 reduce-scatter.4.cloned.1.call-update
  303.3 0.0 all-reduce.13.cloned.1.call-start
  303.3 1.2 copy-done.1
  304.5 0.1 copy-done.4
  304.6 0.2 copy-done.12
  304.8 1.5 fusion.36
  306.4 1.4 fusion.39
  307.8 0.1 stack.102
  307.9 0.1 stack.113
  308.1 0.7 pad_maximum_fusion.2
  308.8 0.0 all-reduce.13.cloned.1.call-update
  308.8 0.0 all-reduce.11.cloned.1.call-start
  308.9 1.6 fusion.55
  310.5 121.4 %reduce-scatter.4.cloned.1.call-done = f32[64,512]{1,0:T(8,128)} async-done(((f32[2048,512]{1,0:T(8,128)}), f32[64,512]{1,0:T(8,128)}) %reduce-scatter.4.cloned.1.call-update) | async-done | bytes 131088
  431.9 1.7 copy.14
  433.6 0.0 all-reduce.11.cloned.1.call-update
  433.7 2.2 fusion.49
  435.9 136.4 %all-reduce.13.cloned.1.call-done = f32[2,9,2048]{2,1,0:T(8,128)} async-done(((f32[2,9,2048]{2,1,0:T(8,128)}), f32[2,9,2048]{2,1,0:T(8,128)}) %all-reduce.13.cloned.1.call-update) | async-done | bytes 147472 | tf_op jit(solution)/shard_map/psum | solution.py:141
  572.3 0.8 constant_dynamic-slice_fusion
  573.1 0.6 copy.12
  573.7 142.5 %all-reduce.11.cloned.1.call-done = f32[64,512]{0,1:T(8,128)} async-done(((f32[64,512]{0,1:T(8,128)}), f32[64,512]{0,1:T(8,128)}) %all-reduce.11.cloned.1.call-update) | async-done | bytes 131088 | tf_op jit(solution)/shard_map/psum | solution.py:108
  716.2 1.7 copy.11
  (33 shorter events, 0.1 us)
Async XLA Ops:
  8.0 15.4 %copy-start = (bf16[1,2,72,256]{3,2,1,0:T(8,128)(2,1)S(1)}, bf16[1,2,72,256]{3,2,1,0:T(8,128)(2,1)}, u32[]{:S(2)}) copy-start(bf16[1,2,72,256]{3,2,1,0:T(8,128)(2,1)} %param.9) | copy-start | bytes 221188
  8.0 17.1 %copy-start.16 = (bf16[2,9,2048]{2,0,1:T(2,128)(2,1)S(1)}, bf16[2,9,2048]{2,0,1:T(2,128)(2,1)}, u32[]{:S(2)}) copy-start(bf16[2,9,2048]{2,0,1:T(2,128)(2,1)} %param.6) | copy-start | bytes 221188
  8.0 423.9 %reduce-scatter.4.cloned.1.call-start = ((), (), s32[]{:S(2)}) async-start(), calls=%async_computation.3 | async-start | bytes 4325376
  8.1 17.1 %copy-start.15 = (bf16[2048,512]{1,0:T(8,128)(2,1)S(1)}, bf16[2048,512]{1,0:T(8,128)(2,1)}, u32[]{:S(2)}) copy-start(bf16[2048,512]{1,0:T(8,128)(2,1)} %param.7) | copy-start | bytes 6291460
  8.1 38.0 %collective-permute-start.2 = (bf16[1,2,72,2048]{3,2,1,0:T(8,128)(2,1)}, bf16[1,2,72,2048]{3,2,1,0:T(8,128)(2,1)S(1)}, u32[]{:S(2)}, u32[]{:S(2)}) collective-permute-start(bf16[1,2,72,2048]{3,2,1,0:T(8,128)(2,1)} %param.5), channel_id=1, source_target_pairs={{0,12},{1,13},{2,14},{3,15},{4,16},{5,17},{6,18},{7,19},{8,20},{9,... | collective-permute-start | bytes 1769480 | tf_op jit(solution)/shard_map/ppermute | solution.py:14
  13.8 19.5 %collective-permute-start.1 = (bf16[1,2,72,2048]{3,2,1,0:T(8,128)(2,1)}, bf16[1,2,72,2048]{3,2,1,0:T(8,128)(2,1)S(1)}, u32[]{:S(2)}, u32[]{:S(2)}) collective-permute-start(bf16[1,2,72,2048]{3,2,1,0:T(8,128)(2,1)} %param.5), channel_id=1, source_target_pairs={{6,0},{7,1},{8,2},{9,3},{10,4},{11,5},{12,6},{13,7},{14,8},{15,9},... | collective-permute-start | bytes 1769480 | tf_op jit(solution)/shard_map/ppermute | solution.py:14
  15.1 29.8 %collective-permute-start = (bf16[1,2,72,2048]{3,2,1,0:T(8,128)(2,1)}, bf16[1,2,72,2048]{3,2,1,0:T(8,128)(2,1)S(1)}, u32[]{:S(2)}, u32[]{:S(2)}) collective-permute-start(bf16[1,2,72,2048]{3,2,1,0:T(8,128)(2,1)} %param.5), channel_id=1, source_target_pairs={{0,6},{1,7},{2,8},{3,9},{4,10},{5,11},{6,12},{7,13},{8,14},{9,15},... | collective-permute-start | bytes 1769480 | tf_op jit(solution)/shard_map/ppermute | solution.py:14
  22.1 50.0 %collective-permute-start.3 = (bf16[1,2,72,2048]{3,2,1,0:T(8,128)(2,1)}, bf16[1,2,72,2048]{3,2,1,0:T(8,128)(2,1)S(1)}, u32[]{:S(2)}, u32[]{:S(2)}) collective-permute-start(bf16[1,2,72,2048]{3,2,1,0:T(8,128)(2,1)} %param.5), channel_id=1, source_target_pairs={{12,0},{13,1},{14,2},{15,3},{16,4},{17,5},{18,6},{19,7},{20,8},{21... | collective-permute-start | bytes 1769480 | tf_op jit(solution)/shard_map/ppermute | solution.py:14
  25.2 19.7 %copy-start.3 = (bf16[1,2,72,2048]{3,2,1,0:T(8,128)(2,1)S(1)}, bf16[1,2,72,2048]{3,2,1,0:T(8,128)(2,1)}, u32[]{:S(2)}) copy-start(bf16[1,2,72,2048]{3,2,1,0:T(8,128)(2,1)} %param.5) | copy-start | bytes 1769476
  33.3 12.8 %copy-start.7 = (bf16[1,2,72,2048]{3,2,1,0:T(8,128)(2,1)}, bf16[1,2,72,2048]{3,2,1,0:T(8,128)(2,1)S(1)}, u32[]{:S(2)}) copy-start(bf16[1,2,72,2048]{3,2,1,0:T(8,128)(2,1)S(1)} %collective-permute-done.1) | copy-start | bytes 1769476
  44.9 1.1 copy-start.11
  46.1 26.8 %copy-start.5 = (bf16[1,2,72,2048]{3,2,1,0:T(8,128)(2,1)}, bf16[1,2,72,2048]{3,2,1,0:T(8,128)(2,1)S(1)}, u32[]{:S(2)}) copy-start(bf16[1,2,72,2048]{3,2,1,0:T(8,128)(2,1)S(1)} %collective-permute-done.2) | copy-start | bytes 1769476
  72.0 0.8 copy-start.9
  72.9 0.8 copy-start.2
  73.7 122.0 %copy-start.17 = (f32[2,2048]{1,0:T(2,128)S(1)}, f32[2,2048]{1,0:T(2,128)}, u32[]{:S(2)}) copy-start(f32[2,2048]{1,0:T(2,128)} %param.8) | copy-start | bytes 49156
  294.1 0.8 copy-start.13
  303.2 1.3 copy-start.1
  303.2 1.4 copy-start.4
  303.2 1.6 copy-start.12
  303.3 269.0 %all-reduce.13.cloned.1.call-start = ((), (), s32[]{:S(2)}) async-start(), calls=%async_computation.2 | async-start | bytes 524288 | tf_op jit(solution)/shard_map/psum | solution.py:141
  304.8 1.5 copy-start.6
  304.8 1.6 copy-start.8
  304.8 1.6 copy-start.10
  307.8 1.1 copy-start.14
  308.8 407.4 %all-reduce.11.cloned.1.call-start = ((), (), s32[]{:S(2)}) async-start(), calls=%async_computation.1 | async-start | bytes 524288 | tf_op jit(solution)/shard_map/psum | solution.py:108
Sparse Core Ops, SparseCore 0:
  303.4 128.4 reduce-scatter.3
Sparse Core Ops, SparseCore 1:
  308.9 263.3 all-reduce.12
  575.1 141.1 all-reduce.10
where the time goes:
time: 726 us; the launch traced here: 725 us
  waiting for transfers between devices  446 us (61%)
  blocking collectives  215 us (30%)
  between operations  15.8 us (2%)
  starting transfers between devices  15.4 us (2%)
  other arithmetic  13.8 us (2%)
  local copies, waits for them, and re-layouts  13.2 us (2%)
    psum x1, waiting for transfers between devices, body(): grad_pw = lax.psum(snapshot_grad, 'dp')  142 us
    psum x1, waiting for transfers between devices, body(): summed = lax.psum(local_grads, ('dp', 'space'))  136 us
    psum x1, blocking collectives, body(): lax.psum((jnp.sum(input_values, axis=(1, 2, 3)), jnp.sum(input_values * i...  122 us
    unnamed x4, waiting for transfers between devices  121 us
    psum x1, blocking collectives, body(): lax.psum((jnp.sum(normalized_gradient, axis=(1, 2, 3)), jnp.sum(normalize...  93.1 us
    ppermute x4, waiting for transfers between devices, shifted(): lax.ppermute(value, axis, [(source, source + steps) for source in range(l...  45.1 us
    ppermute x4, starting transfers between devices, shifted(): lax.ppermute(value, axis, [(source, source + steps) for source in range(l...  15.3 us
  transfers between devices with their start and end apart: 7, of which 6 were waited for; matrix products, arithmetic and copies ran while one was open for 2% of the time, Pallas kernels for 0%

commit v1 on v0

--- a/solution.py
+++ b/solution.py
@@ -105,7 +105,7 @@
     snapshot_grad = lax.psum_scatter(
         jnp.concatenate(pieces, axis=1), "space", scatter_dimension=0, tiled=True
     )
-    grad_pw = lax.psum(snapshot_grad, "dp")
+    grad_pw = lax.all_gather(snapshot_grad, "dp").sum(axis=0)
     grad_used = jnp.stack(
         [
             lax.dot_general(

time: 726 us -> 587 us (0.81)
  the two profiles are of different devices: /device:TPU:2 before, /device:TPU:1 now
where the time goes in v1:
time: 587 us; the launch traced here: 586 us
  waiting for transfers between devices  306 us (52%)
  blocking collectives  214 us (36%)
  starting transfers between devices  16.5 us (3%)
  other arithmetic  16.2 us (3%)
  between operations  15.8 us (3%)
  local copies, waits for them, and re-layouts  9.83 us (2%)
  matrix products  6.94 us (1%)
    psum x1, waiting for transfers between devices, body(): summed = lax.psum(local_grads, ('dp', 'space'))  142 us
    psum x1, blocking collectives, body(): lax.psum((jnp.sum(input_values, axis=(1, 2, 3)), jnp.sum(input_values * i...  120 us
    reduce_scatter x1, waiting for transfers between devices, body(): lax.psum_scatter(jnp.concatenate(pieces, axis=1), 'space', scatter_dimens...  119 us
    psum x1, blocking collectives, body(): lax.psum((jnp.sum(normalized_gradient, axis=(1, 2, 3)), jnp.sum(normalize...  94.3 us
    ppermute x4, waiting for transfers between devices, shifted(): lax.ppermute(value, axis, [(source, source + steps) for source in range(l...  45.5 us
    ppermute x4, starting transfers between devices, shifted(): lax.ppermute(value, axis, [(source, source + steps) for source in range(l...  16.3 us
  transfers between devices with their start and end apart: 7, of which 5 were waited for; matrix products, arithmetic and copies ran while one was open for 2% of the time, Pallas kernels for 0%

profile of v1, /device:TPU:1, one launch (start us, length us, event | category | flops | bytes accessed | tf_op | source)
XLA Modules:
  0.0 585.9 jit_solution(15378630568215255059)
XLA Ops:
  8.0 0.0 copy-start
  8.0 0.0 reduce-scatter.4.cloned.1.call-start
  8.1 0.0 copy-start.15
  8.1 6.2 %collective-permute-start.2 = (bf16[1,2,72,2048]{3,2,1,0:T(8,128)(2,1)}, bf16[1,2,72,2048]{3,2,1,0:T(8,128)(2,1)S(1)}, u32[]{:S(2)}, u32[]{:S(2)}) collective-permute-start(bf16[1,2,72,2048]{3,2,1,0:T(8,128)(2,1)} %param.5), channel_id=1, source_target_pairs={{0,12},{1,13},{2,14},{3,15},{4,16},{5,17},{6,18},{7,19},{8,20},{9,... | collective-permute-start | bytes 1769480 | tf_op jit(solution)/shard_map/ppermute | solution.py:14
  14.3 1.3 collective-permute-start.1
  15.6 7.5 %collective-permute-start = (bf16[1,2,72,2048]{3,2,1,0:T(8,128)(2,1)}, bf16[1,2,72,2048]{3,2,1,0:T(8,128)(2,1)S(1)}, u32[]{:S(2)}, u32[]{:S(2)}) collective-permute-start(bf16[1,2,72,2048]{3,2,1,0:T(8,128)(2,1)} %param.5), channel_id=1, source_target_pairs={{0,6},{1,7},{2,8},{3,9},{4,10},{5,11},{6,12},{7,13},{8,14},{9,15},... | collective-permute-start | bytes 1769480 | tf_op jit(solution)/shard_map/ppermute | solution.py:14
  23.1 1.3 collective-permute-start.3
  24.5 1.7 convolution_bitcast_fusion
  26.2 0.1 slice_convert_fusion.17
  26.3 0.0 copy-start.3
  26.3 0.5 convolution_bitcast_fusion.1
  26.8 7.0 %collective-permute-done.1 = bf16[1,2,72,2048]{3,2,1,0:T(8,128)(2,1)S(1)} collective-permute-done((bf16[1,2,72,2048]{3,2,1,0:T(8,128)(2,1)}, bf16[1,2,72,2048]{3,2,1,0:T(8,128)(2,1)S(1)}, u32[]{:S(2)}, u32[]{:S(2)}) %collective-permute-start.1) | collective-permute-done | bytes 589856 | tf_op jit(solution)/shard_map/ppermute | solution.py:14
  33.8 9.0 %collective-permute-done = bf16[1,2,72,2048]{3,2,1,0:T(8,128)(2,1)S(1)} collective-permute-done((bf16[1,2,72,2048]{3,2,1,0:T(8,128)(2,1)}, bf16[1,2,72,2048]{3,2,1,0:T(8,128)(2,1)S(1)}, u32[]{:S(2)}, u32[]{:S(2)}) %collective-permute-start) | collective-permute-done | bytes 589856 | tf_op jit(solution)/shard_map/ppermute | solution.py:14
  42.8 1.1 fusion.58
  44.0 29.5 %collective-permute-done.3 = bf16[1,2,72,2048]{3,2,1,0:T(8,128)(2,1)S(1)} collective-permute-done((bf16[1,2,72,2048]{3,2,1,0:T(8,128)(2,1)}, bf16[1,2,72,2048]{3,2,1,0:T(8,128)(2,1)S(1)}, u32[]{:S(2)}, u32[]{:S(2)}) %collective-permute-start.3) | collective-permute-done | bytes 589856 | tf_op jit(solution)/shard_map/ppermute | solution.py:14
  73.5 0.8 fusion.57
  74.3 0.8 copy-done.2
  75.2 0.4 convert_reduce_fusion
  75.5 120.0 %all-reduce.7 = (f32[2,2048]{1,0:T(2,128)S(1)}, f32[2,2048]{1,0:T(2,128)S(1)}) all-reduce(f32[2,2048]{1,0:T(2,128)S(1)} %get-tuple-element.39, f32[2,2048]{1,0:T(2,128)S(1)} %get-tuple-element.38), channel_id=1, replica_groups=mesh['dp'=16,'space'=32] {'dp','space'}, use_global_device_ids=true, to_apply=%region_3.4 | all-reduce | flops 8192 | bytes 65536 | tf_op jit(solution)/shard_map/psum | solution.py:77
  195.6 2.0 fusion.61
  197.6 94.3 %all-reduce.6 = (f32[2,2048]{1,0:T(2,128)S(1)}, f32[2,2048]{1,0:T(2,128)S(1)}) all-reduce(f32[2,2048]{1,0:T(2,128)S(1)} %get-tuple-element.10, f32[2,2048]{1,0:T(2,128)S(1)} %get-tuple-element.9), channel_id=1, replica_groups=mesh['dp'=16,'space'=32] {'dp','space'}, use_global_device_ids=true, to_apply=%region_9.10 | all-reduce | flops 8192 | bytes 65536 | tf_op jit(solution)/shard_map/psum | solution.py:122
  291.9 3.2 fusion.10
  295.2 0.1 fusion.62
  295.3 0.5 fusion.64
  295.8 0.3 copy-done.13
  296.1 0.5 fusion.63
  296.6 2.5 pad_maximum_fusion
  299.0 5.3 copy.12
  304.4 0.0 reduce-scatter.4.cloned.1.call-update
  304.4 0.0 all-reduce.10.cloned.1.call-start
  304.5 1.2 copy-done.1
  305.7 0.1 copy-done.4
  305.8 0.2 copy-done.12
  306.0 1.5 fusion.36
  307.6 1.4 fusion.39
  309.0 0.1 stack.102
  309.1 0.1 stack.113
  309.2 0.7 pad_maximum_fusion.2
  310.0 0.0 all-reduce.10.cloned.1.call-update
  310.0 0.0 all-gather.3.cloned.1.call-start
  310.0 118.7 %reduce-scatter.4.cloned.1.call-done = f32[64,512]{1,0:T(8,128)} async-done(((f32[2048,512]{1,0:T(8,128)}), f32[64,512]{1,0:T(8,128)}) %reduce-scatter.4.cloned.1.call-update) | async-done | bytes 131088 | tf_op jit(solution)/shard_map/reduce_scatter | solution.py:105
  428.8 0.0 all-gather.3.cloned.1.call-update
  428.8 1.6 fusion.55
  430.4 2.2 fusion.49
  432.6 142.0 %all-reduce.10.cloned.1.call-done = f32[2,9,2048]{2,1,0:T(8,128)} async-done(((f32[2,9,2048]{2,1,0:T(8,128)}), f32[2,9,2048]{2,1,0:T(8,128)}) %all-reduce.10.cloned.1.call-update) | async-done | bytes 147472 | tf_op jit(solution)/shard_map/psum | solution.py:141
  574.6 0.8 constant_dynamic-slice_fusion
  575.4 0.6 copy.11
  576.0 2.4 reduce_sum.209
  (32 shorter events, 0.1 us)
Async XLA Ops:
  8.0 16.5 %copy-start = (bf16[1,2,72,256]{3,2,1,0:T(8,128)(2,1)S(1)}, bf16[1,2,72,256]{3,2,1,0:T(8,128)(2,1)}, u32[]{:S(2)}) copy-start(bf16[1,2,72,256]{3,2,1,0:T(8,128)(2,1)} %param.9) | copy-start | bytes 221188
  8.0 18.2 %copy-start.16 = (bf16[2,9,2048]{2,0,1:T(2,128)(2,1)S(1)}, bf16[2,9,2048]{2,0,1:T(2,128)(2,1)}, u32[]{:S(2)}) copy-start(bf16[2,9,2048]{2,0,1:T(2,128)(2,1)} %param.6) | copy-start | bytes 221188
  8.0 420.7 %reduce-scatter.4.cloned.1.call-start = ((), (), s32[]{:S(2)}) async-start(), calls=%async_computation.3 | async-start | bytes 4325376 | tf_op jit(solution)/shard_map/reduce_scatter | solution.py:105
  8.1 18.2 %copy-start.15 = (bf16[2048,512]{1,0:T(8,128)(2,1)S(1)}, bf16[2048,512]{1,0:T(8,128)(2,1)}, u32[]{:S(2)}) copy-start(bf16[2048,512]{1,0:T(8,128)(2,1)} %param.7) | copy-start | bytes 6291460
  8.1 35.9 %collective-permute-start.2 = (bf16[1,2,72,2048]{3,2,1,0:T(8,128)(2,1)}, bf16[1,2,72,2048]{3,2,1,0:T(8,128)(2,1)S(1)}, u32[]{:S(2)}, u32[]{:S(2)}) collective-permute-start(bf16[1,2,72,2048]{3,2,1,0:T(8,128)(2,1)} %param.5), channel_id=1, source_target_pairs={{0,12},{1,13},{2,14},{3,15},{4,16},{5,17},{6,18},{7,19},{8,20},{9,... | collective-permute-start | bytes 1769480 | tf_op jit(solution)/shard_map/ppermute | solution.py:14
  14.3 19.5 %collective-permute-start.1 = (bf16[1,2,72,2048]{3,2,1,0:T(8,128)(2,1)}, bf16[1,2,72,2048]{3,2,1,0:T(8,128)(2,1)S(1)}, u32[]{:S(2)}, u32[]{:S(2)}) collective-permute-start(bf16[1,2,72,2048]{3,2,1,0:T(8,128)(2,1)} %param.5), channel_id=1, source_target_pairs={{6,0},{7,1},{8,2},{9,3},{10,4},{11,5},{12,6},{13,7},{14,8},{15,9},... | collective-permute-start | bytes 1769480 | tf_op jit(solution)/shard_map/ppermute | solution.py:14
  15.6 27.2 %collective-permute-start = (bf16[1,2,72,2048]{3,2,1,0:T(8,128)(2,1)}, bf16[1,2,72,2048]{3,2,1,0:T(8,128)(2,1)S(1)}, u32[]{:S(2)}, u32[]{:S(2)}) collective-permute-start(bf16[1,2,72,2048]{3,2,1,0:T(8,128)(2,1)} %param.5), channel_id=1, source_target_pairs={{0,6},{1,7},{2,8},{3,9},{4,10},{5,11},{6,12},{7,13},{8,14},{9,15},... | collective-permute-start | bytes 1769480 | tf_op jit(solution)/shard_map/ppermute | solution.py:14
  23.1 50.3 %collective-permute-start.3 = (bf16[1,2,72,2048]{3,2,1,0:T(8,128)(2,1)}, bf16[1,2,72,2048]{3,2,1,0:T(8,128)(2,1)S(1)}, u32[]{:S(2)}, u32[]{:S(2)}) collective-permute-start(bf16[1,2,72,2048]{3,2,1,0:T(8,128)(2,1)} %param.5), channel_id=1, source_target_pairs={{12,0},{13,1},{14,2},{15,3},{16,4},{17,5},{18,6},{19,7},{20,8},{21... | collective-permute-start | bytes 1769480 | tf_op jit(solution)/shard_map/ppermute | solution.py:14
  26.3 16.5 %copy-start.3 = (bf16[1,2,72,2048]{3,2,1,0:T(8,128)(2,1)S(1)}, bf16[1,2,72,2048]{3,2,1,0:T(8,128)(2,1)}, u32[]{:S(2)}) copy-start(bf16[1,2,72,2048]{3,2,1,0:T(8,128)(2,1)} %param.5) | copy-start | bytes 1769476
  33.8 10.1 %copy-start.7 = (bf16[1,2,72,2048]{3,2,1,0:T(8,128)(2,1)}, bf16[1,2,72,2048]{3,2,1,0:T(8,128)(2,1)S(1)}, u32[]{:S(2)}) copy-start(bf16[1,2,72,2048]{3,2,1,0:T(8,128)(2,1)S(1)} %collective-permute-done.1) | copy-start | bytes 1769476
  42.8 1.1 copy-start.11
  44.0 30.4 %copy-start.5 = (bf16[1,2,72,2048]{3,2,1,0:T(8,128)(2,1)}, bf16[1,2,72,2048]{3,2,1,0:T(8,128)(2,1)S(1)}, u32[]{:S(2)}) copy-start(bf16[1,2,72,2048]{3,2,1,0:T(8,128)(2,1)S(1)} %collective-permute-done.2) | copy-start | bytes 1769476
  73.5 0.8 copy-start.9
  74.3 0.8 copy-start.2
  75.2 120.4 %copy-start.17 = (f32[2,2048]{1,0:T(2,128)S(1)}, f32[2,2048]{1,0:T(2,128)}, u32[]{:S(2)}) copy-start(f32[2,2048]{1,0:T(2,128)} %param.8) | copy-start | bytes 49156
  295.3 0.8 copy-start.13
  304.4 1.3 copy-start.1
  304.4 1.4 copy-start.4
  304.4 1.6 copy-start.12
  304.4 270.2 %all-reduce.10.cloned.1.call-start = ((), (), s32[]{:S(2)}) async-start(), calls=%async_computation.1 | async-start | bytes 524288 | tf_op jit(solution)/shard_map/psum | solution.py:141
  306.0 1.5 copy-start.6
  306.0 1.6 copy-start.8
  306.0 1.6 copy-start.10
  309.0 119.8 %copy-start.14 = (bf16[1,1,2,72,2048]{4,3,2,1,0:T(8,128)(2,1)S(1)}, bf16[1,1,2,72,2048]{4,3,2,1,0:T(8,128)(2,1)}, u32[]{:S(2)}) copy-start(bf16[1,1,2,72,2048]{4,3,2,1,0:T(8,128)(2,1)} %copy-done.13) | copy-start | bytes 1769476
  310.0 266.1 %all-gather.3.cloned.1.call-start = ((), (), s32[]{:S(2)}) async-start(), calls=%async_computation.2 | async-start | bytes 2228224 | tf_op jit(solution)/shard_map/all_gather | solution.py:108
Sparse Core Ops, SparseCore 0:
  304.5 124.1 reduce-scatter.3
  430.8 69.7 all-gather.2
Sparse Core Ops, SparseCore 1:
  310.1 264.5 all-reduce.9
